TPU v7x, 32 devices: a whole 2x2x4 slice. The times are simulated.
32 devices in a mesh: group: 1, dev: 32 (over z, y, x, core).
Axes of the slice: x: 2, y: 2, z: 4, core: 2. Of those that a mesh axis runs over, the one named last changes fastest.
Arguments:
- traces: bfloat16 [2048, 1024], P(('group', 'dev')), may hold values from -6 to 6
- fetch_rows: int32 [1, 32768], P('group', 'dev'), may hold values from 0 to 2047, as said below
- pair_left: int32 [1, 1024, 32], P('group', 'dev'), may hold values from 0 to 1023
- pair_right: int32 [1, 1024, 32], P('group', 'dev'), may hold values from 0 to 1023
- taper_index: int32 [1, 1024, 32], P('group', 'dev'), may hold values from 0 to 15
- taper_table: float32 [16], replicated, may hold values from 0.1 to 1
Outputs:
- predicted: float32 [1024, 1024], P('dev', 'group')
Inputs may be any that keep to these rules, and one draw needn't show every extreme that they name: `fetch_rows`: entry j of device d's block of 1024 entries (columns d * 1024 to (d + 1) * 1024 - 1) names a trace held by device j // 32 of the group: it lies in [(j // 32) * 64, (j // 32 + 1) * 64). So every device lists exactly 32 traces of each device of its group.
All inputs are finite; a program needn't handle non-finite values.
Results may differ from a plain program's by a relative error of at most 0.0003.
Values may be sent and summed in bfloat16 or wider, within the bound.
No kernel may reach another device: no remote copies, remote signals or barrier semaphores. Data moves between devices by JAX's collectives and lax.ppermute only.
A program may use at most 64 MiB of HBM per device.

v0:
```python
import functools

import jax
import jax.numpy as jnp
from jax import lax
from jax.experimental import pallas as pl
from jax.experimental.pallas import tpu as pltpu
from jax.sharding import PartitionSpec as P


LANES = 128
ROWS = 8
PER_STEP = 4
WORK_BYTES = 16 << 20


def exchange(value, count, even, odd=None):
    odd = even if odd is None else odd
    return lax.ppermute(value, "dev", [(i, i ^ (odd if i & 1 else even)) for i in range(count)])


def gather_blocks(own, count):
    levels = {0: own}
    fars = []
    pieces = []

    def level_of(level):
        if level not in levels:
            low = level & -level
            levels[level] = exchange(level_of(level ^ low), count, 8 * low)
        return levels[level]

    for level in range(count // 8):
        near = exchange(level_of(level), count, 2, 4)
        both = jnp.concatenate([level_of(level), near], axis=0)
        far = exchange(fars[0], count, 8) if level == 1 else exchange(both, count, 4, 2)
        fars.append(far)
        pieces.append((both, 4 * level))
        pieces.append((far, 4 * level + 2))
        pieces.append((exchange(both, count, 1), count // 2 + 4 * level))
        pieces.append((exchange(far, count, 1), count // 2 + 4 * level + 2))
    return pieces


def slots_of(rows, rows_each, count):
    owner = rows // rows_each
    offset = owner ^ lax.axis_index("dev")
    plane = (offset >> 1) & 3
    swapped = ((plane & 1) << 1) | (plane >> 1)
    label = jnp.where(owner % 2 == 0, plane, swapped)
    slot = (offset & 1) * (count // 2) + (offset >> 3) * 4 + label
    return slot, rows % rows_each


def aperture_kernel(slots, places, tapers, table, *refs, aperture, blocks, outs, scale):
    pieces = refs[: len(slots)]
    out_ref, held, left, right, products, weights, sems = refs[len(slots) :]
    copies = []
    for i, (piece, slot) in enumerate(zip(pieces, slots, strict=True)):
        copies.append(pltpu.make_async_copy(piece, held.at[pl.ds(slot, piece.shape[0])], sems.at[i]))
        copies[-1].start()
    lane = lax.broadcasted_iota(jnp.int32, (ROWS, LANES), 1)
    row = lax.broadcasted_iota(jnp.int32, (ROWS, LANES), 0)
    tile = ROWS * blocks
    half = LANES // 2
    index = tapers[...]
    chosen = jnp.zeros(index.shape, jnp.float32)
    for j in range(table.shape[0]):
        chosen = jnp.where(index == j, table[j], chosen)
    weights[...] = jnp.concatenate([chosen] * blocks, axis=1)
    for copy in copies:
        copy.wait()

    def shifted(tiles, amount, carried, **how):
        rolled = [pltpu.roll(t, amount, 1, **how) for t in tiles]
        before = [jnp.zeros((ROWS, LANES), jnp.float32)] + rolled[:-1]
        return [jnp.where(carried, b, r) for b, r in zip(before, rolled, strict=True)]

    def columns(ref, p):
        parts = [ref[pl.ds(tile * g + p, ROWS, stride=blocks), :] for g in range(aperture // ROWS)]
        return jnp.concatenate(parts, axis=0).astype(jnp.bfloat16)

    def toeplitz(source, n, depth):
        none = jnp.zeros((aperture, LANES), jnp.bfloat16)
        pick = lambda i: source[i] if i >= 0 else none
        rows = [jnp.concatenate([pick(n - p), pick(n + 1 - p)], axis=1) for p in range(depth)]
        return jnp.concatenate(rows, axis=0)

    def multiply(o, left_ref, right_ref, product_ref):
        left_places = places.at[0, pl.ds(o * aperture, aperture)]
        right_places = places.at[0, pl.ds((outs + o) * aperture, aperture)]
        for k in range(aperture):
            here = pl.ds(blocks * k, blocks)
            left_ref[here, :] = held[left_places[k]].astype(jnp.float32)
            right_ref[here, :] = held[right_places[k]].astype(jnp.float32)
        even = [columns(right_ref, p) for p in range(blocks)]
        late = jnp.concatenate(
            [jnp.zeros((aperture, half), jnp.bfloat16), jnp.concatenate(even, axis=1)[:, :-half]], axis=1
        )
        odd = [late[:, LANES * p : LANES * (p + 1)] for p in range(blocks)]
        lhs = jnp.concatenate([columns(left_ref, p) for p in range(blocks)], axis=0).T
        lhs = lhs.astype(jnp.float32) * weights[pl.ds(o, 1), :]
        high = lhs.astype(jnp.bfloat16)
        low = (lhs - high.astype(jnp.float32)).astype(jnp.bfloat16)
        for n in range(0, blocks, 2):
            depth = blocks // 2 if n + 2 <= blocks // 2 else blocks
            wide = depth * aperture
            factor = jnp.concatenate(
                [jnp.concatenate([term[:half, :wide], term[half:, :wide]], axis=1) for term in (high, low)], axis=0
            )
            delayed = jnp.concatenate([toeplitz(even, n, depth), toeplitz(odd, n, depth)], axis=0)
            both = jnp.dot(factor, delayed, preferred_element_type=jnp.float32)
            product_ref[:, pl.ds(n * LANES, 2 * LANES)] = both[:half] + both[half:]

    def add_up(o, product_ref):
        def tiles(g):
            return [product_ref[pl.ds(ROWS * g, ROWS), pl.ds(v * LANES, LANES)] for v in range(blocks)]

        total = tiles(half // ROWS - 1)
        for g in range(half // ROWS - 2, -1, -1):
            moved = shifted(total, ROWS, lane < ROWS)
            total = [m + t for m, t in zip(moved, tiles(g), strict=True)]
        total = shifted(total, 0, lane < row, stride=1, stride_axis=0)
        sums = jnp.concatenate([jnp.sum(t, axis=0, keepdims=True) for t in total], axis=1)
        out_ref[pl.ds(o, 1), :] = sums * scale

    def multiply_all(i):
        for u in range(PER_STEP):
            multiply(i * PER_STEP + u, left.at[u], right.at[u], products.at[u])

    def add_up_all(i):
        for u in range(PER_STEP):
            add_up(i * PER_STEP + u, products.at[u])

    def step(i, carry):
        add_up_all(i - 1)
        multiply_all(i)
        return carry

    multiply_all(0)
    lax.fori_loop(1, outs // PER_STEP, step, 0)
    add_up_all(outs // PER_STEP - 1)


def aperture_sums(places, tapers, table, pieces, rows_each, scale):
    outs, aperture = tapers.shape
    blocks = pieces[0][0].shape[1]
    held = sum(piece.shape[0] for piece, _ in pieces)
    work = pltpu.VMEM((PER_STEP, aperture * blocks, LANES), jnp.float32)
    scalars, vectors = pl.BlockSpec(memory_space=pltpu.SMEM), pl.BlockSpec(memory_space=pltpu.VMEM)
    held_bytes = held * blocks * LANES * 2
    return pl.pallas_call(
        functools.partial(
            aperture_kernel,
            [slot * rows_each for _, slot in pieces],
            aperture=aperture,
            blocks=blocks,
            outs=outs,
            scale=scale,
        ),
        out_shape=jax.ShapeDtypeStruct((outs, blocks * LANES), jnp.float32),
        in_specs=[scalars, vectors, scalars] + [pl.BlockSpec(memory_space=pl.ANY)] * len(pieces),
        out_specs=vectors,
        scratch_shapes=[
            pltpu.VMEM((held, blocks, LANES), jnp.bfloat16),
            work,
            work,
            pltpu.VMEM((PER_STEP, LANES // 2, blocks * LANES), jnp.float32),
            pltpu.VMEM((outs, aperture * blocks), jnp.float32),
            pltpu.SemaphoreType.DMA((len(pieces),)),
        ],
        compiler_params=pltpu.CompilerParams(vmem_limit_bytes=held_bytes + WORK_BYTES),
        name="aperture_sums",
    )(places, tapers, table, *[piece for piece, _ in pieces])


def shards(traces, fetch_rows, pair_left, pair_right, taper_index, taper_table):
    rows_each, samples = traces.shape
    count = lax.axis_size("dev")
    _, aperture = pair_left.shape[1:]
    pieces = gather_blocks(traces.reshape(rows_each, samples // LANES, LANES), count)

    slot, row = slots_of(fetch_rows, rows_each, count)
    digits = jnp.concatenate([slot, row], axis=0).astype(jnp.bfloat16)
    wanted = jnp.concatenate([pair_left.reshape(1, -1), pair_right.reshape(1, -1)], axis=1)
    listed = lax.broadcasted_iota(jnp.int32, (digits.shape[1], wanted.shape[1]), 0)
    found = jnp.dot(digits, (listed == wanted).astype(jnp.bfloat16), preferred_element_type=jnp.float32)
    places = (found[:1] * rows_each + found[1:]).astype(jnp.int32)

    scale = float(1.0 / (samples * aperture * lax.axis_size("group")) ** 0.5)
    partial = aperture_sums(places, taper_index[0], taper_table, pieces, rows_each, scale)
    return lax.psum_scatter(partial, "group", scatter_dimension=1, tiled=True)


def solution(mesh):
    return jax.shard_map(
        shards,
        mesh=mesh,
        in_specs=(
            P(("group", "dev"), None),
            P("group", "dev"),
            P("group", "dev", None),
            P("group", "dev", None),
            P("group", "dev", None),
            P(),
        ),
        out_specs=P("dev", "group"),
        check_vma=False,
    )
```

profile of v0, /device:TPU:0, one launch (start us, length us, event | category | flops | bytes accessed | tf_op | source)
XLA Modules:
  0.0 46.9 jit_solution(9716094465472430018)
XLA Ops:
  0.0 1.0 %copy.7 = bf16[8,8,8,128]{3,2,1,0:T(8,128)(2,1)S(1)} copy(bf16[8,8,8,128]{3,1,2,0:T(8,128)(2,1)} %bitcast.9) | data formatting | bytes 262144
  1.0 4.1 %collective-permute-start.9 = (bf16[64,8,128]{2,1,0:T(8,128)(2,1)S(1)}, bf16[64,8,128]{2,1,0:T(8,128)(2,1)S(1)}, u32[]{:S(2)}, u32[]{:S(2)}) collective-permute-start(bf16[64,8,128]{2,1,0:T(8,128)(2,1)S(1)} %bitcast.5), channel_id=1, source_target_pairs={{0,16},{1,17},{2,18},{3,19},{4,20},{5,21},{6,22},{7,23},{8,24},{9,... | collective-permute-start | bytes 393224 | tf_op jit(solution)/shard_map/ppermute | solution.py:19
  5.1 1.6 %collective-permute-start.4 = (bf16[64,8,128]{2,1,0:T(8,128)(2,1)S(1)}, bf16[64,8,128]{2,1,0:T(8,128)(2,1)S(1)}, u32[]{:S(2)}, u32[]{:S(2)}) collective-permute-start(bf16[64,8,128]{2,1,0:T(8,128)(2,1)S(1)} %bitcast.6), channel_id=1, source_target_pairs={{0,8},{1,9},{2,10},{3,11},{4,12},{5,13},{6,14},{7,15},{8,0},{9,1},... | collective-permute-start | bytes 393224 | tf_op jit(solution)/shard_map/ppermute | solution.py:19
  6.7 1.5 %collective-permute-start = (bf16[64,8,128]{2,1,0:T(8,128)(2,1)S(1)}, bf16[64,8,128]{2,1,0:T(8,128)(2,1)S(1)}, u32[]{:S(2)}, u32[]{:S(2)}) collective-permute-start(bf16[64,8,128]{2,1,0:T(8,128)(2,1)S(1)} %bitcast.7), channel_id=1, source_target_pairs={{0,2},{1,5},{2,0},{3,7},{4,6},{5,1},{6,4},{7,3},{8,10},{9,13},{10,... | collective-permute-start | bytes 393224 | tf_op jit(solution)/shard_map/ppermute | solution.py:19
  8.2 0.1 add_convert_fusion
  8.3 0.1 reshape.9
  8.4 0.1 reshape.10
  8.4 3.2 %collective-permute-done = bf16[64,8,128]{2,1,0:T(8,128)(2,1)S(1)} collective-permute-done((bf16[64,8,128]{2,1,0:T(8,128)(2,1)S(1)}, bf16[64,8,128]{2,1,0:T(8,128)(2,1)S(1)}, u32[]{:S(2)}, u32[]{:S(2)}) %collective-permute-start) | collective-permute-done | bytes 131104 | tf_op jit(solution)/shard_map/ppermute | solution.py:19
  11.7 0.1 collective-permute-start.2
  11.8 1.6 %collective-permute-start.1 = (bf16[128,8,128]{2,1,0:T(8,128)(2,1)S(1)}, bf16[128,8,128]{2,1,0:T(8,128)(2,1)S(1)}, u32[]{:S(2)}, u32[]{:S(2)}) collective-permute-start(bf16[128,8,128]{2,1,0:T(8,128)(2,1)S(1)} %constant_dynamic-update-slice_fusion.refs_0_), channel_id=1, source_target_pairs={{0,4},{1,3},{2,6},{3,1},{4,0},{5,7},{6,2},{7,5},{8,12},{9,11},{10,... | collective-permute-start | bytes 786440 | tf_op jit(solution)/shard_map/ppermute | solution.py:19
  13.3 0.0 collective-permute-done.9
  13.3 0.5 collective-permute-start.14
  13.8 1.5 %collective-permute-start.10 = (bf16[64,8,128]{2,1,0:T(8,128)(2,1)S(1)}, bf16[64,8,128]{2,1,0:T(8,128)(2,1)S(1)}, u32[]{:S(2)}, u32[]{:S(2)}) collective-permute-start(bf16[64,8,128]{2,1,0:T(8,128)(2,1)S(1)} %collective-permute-done.9), channel_id=1, source_target_pairs={{0,2},{1,5},{2,0},{3,7},{4,6},{5,1},{6,4},{7,3},{8,10},{9,13},{10,... | collective-permute-start | bytes 393224 | tf_op jit(solution)/shard_map/ppermute | solution.py:19
  15.3 0.0 collective-permute-done.4
  15.3 0.5 %collective-permute-start.5 = (bf16[64,8,128]{2,1,0:T(8,128)(2,1)S(1)}, bf16[64,8,128]{2,1,0:T(8,128)(2,1)S(1)}, u32[]{:S(2)}, u32[]{:S(2)}) collective-permute-start(bf16[64,8,128]{2,1,0:T(8,128)(2,1)S(1)} %collective-permute-done.4), channel_id=1, source_target_pairs={{0,2},{1,5},{2,0},{3,7},{4,6},{5,1},{6,4},{7,3},{8,10},{9,13},{10,... | collective-permute-start | bytes 393224 | tf_op jit(solution)/shard_map/ppermute | solution.py:19
  15.9 3.2 %collective-permute-done.10 = bf16[64,8,128]{2,1,0:T(8,128)(2,1)S(1)} collective-permute-done((bf16[64,8,128]{2,1,0:T(8,128)(2,1)S(1)}, bf16[64,8,128]{2,1,0:T(8,128)(2,1)S(1)}, u32[]{:S(2)}, u32[]{:S(2)}) %collective-permute-start.10) | collective-permute-done | bytes 131104 | tf_op jit(solution)/shard_map/ppermute | solution.py:19
  19.1 0.2 collective-permute-start.12
  19.2 0.0 collective-permute-done.14
  19.2 1.5 %collective-permute-start.15 = (bf16[64,8,128]{2,1,0:T(8,128)(2,1)S(1)}, bf16[64,8,128]{2,1,0:T(8,128)(2,1)S(1)}, u32[]{:S(2)}, u32[]{:S(2)}) collective-permute-start(bf16[64,8,128]{2,1,0:T(8,128)(2,1)S(1)} %collective-permute-done.14), channel_id=1, source_target_pairs={{0,2},{1,5},{2,0},{3,7},{4,6},{5,1},{6,4},{7,3},{8,10},{9,13},{10,... | collective-permute-start | bytes 393224 | tf_op jit(solution)/shard_map/ppermute | solution.py:19
  20.7 1.6 %collective-permute-start.11 = (bf16[128,8,128]{2,1,0:T(8,128)(2,1)S(1)}, bf16[128,8,128]{2,1,0:T(8,128)(2,1)S(1)}, u32[]{:S(2)}, u32[]{:S(2)}) collective-permute-start(bf16[128,8,128]{2,1,0:T(8,128)(2,1)S(1)} %constant_dynamic-update-slice_fusion.4.refs_8_), channel_id=1, source_target_pairs={{0,4},{1,3},{2,6},{3,1},{4,0},{5,7},{6,2},{7,5},{8,12},{9,11},{10,... | collective-permute-start | bytes 786440 | tf_op jit(solution)/shard_map/ppermute | solution.py:19
  22.4 2.5 %collective-permute-done.15 = bf16[64,8,128]{2,1,0:T(8,128)(2,1)S(1)} collective-permute-done((bf16[64,8,128]{2,1,0:T(8,128)(2,1)S(1)}, bf16[64,8,128]{2,1,0:T(8,128)(2,1)S(1)}, u32[]{:S(2)}, u32[]{:S(2)}) %collective-permute-start.15) | collective-permute-done | bytes 131104 | tf_op jit(solution)/shard_map/ppermute | solution.py:19
  24.9 1.8 %collective-permute-start.16 = (bf16[128,8,128]{2,1,0:T(8,128)(2,1)S(1)}, bf16[128,8,128]{2,1,0:T(8,128)(2,1)S(1)}, u32[]{:S(2)}, u32[]{:S(2)}) collective-permute-start(bf16[128,8,128]{2,1,0:T(8,128)(2,1)S(1)} %constant_dynamic-update-slice_fusion.6.refs_12_), channel_id=1, source_target_pairs={{0,4},{1,3},{2,6},{3,1},{4,0},{5,7},{6,2},{7,5},{8,12},{9,11},{10,... | collective-permute-start | bytes 786440 | tf_op jit(solution)/shard_map/ppermute | solution.py:19
  26.6 1.6 %collective-permute-start.6 = (bf16[128,8,128]{2,1,0:T(8,128)(2,1)S(1)}, bf16[128,8,128]{2,1,0:T(8,128)(2,1)S(1)}, u32[]{:S(2)}, u32[]{:S(2)}) collective-permute-start(bf16[128,8,128]{2,1,0:T(8,128)(2,1)S(1)} %collective-permute-done.1.refs_1_), channel_id=1, source_target_pairs={{0,8},{1,9},{2,10},{3,11},{4,12},{5,13},{6,14},{7,15},{8,0},{9,1},... | collective-permute-start | bytes 786440 | tf_op jit(solution)/shard_map/ppermute | solution.py:19
  28.2 1.5 %fusion = f32[2,2048]{1,0:T(2,128)S(1)} fusion(s32[2048]{0:T(1024)S(1)} %bitcast.10, bf16[1,1024]{1,0:T(2,128)(2,1)S(1)} %fusion.3, bf16[1,1024]{1,0:T(2,128)(2,1)S(1)} %get-tuple-element.5), kind=kOutput, calls=%fused_computation.1 | convolution fusion | flops 10493952 | bytes 28672 | tf_op jit(solution)/shard_map/dot_general | solution.py:187
  29.7 0.1 collective-permute-start.17
  29.9 0.4 collective-permute-start.3
  30.2 0.1 collective-permute-start.13
  30.4 4.7 %collective-permute-done.6.refs_5_ = bf16[128,8,128]{2,1,0:T(8,128)(2,1)S(1)} collective-permute-done((bf16[128,8,128]{2,1,0:T(8,128)(2,1)S(1)}, bf16[128,8,128]{2,1,0:T(8,128)(2,1)S(1)}, u32[]{:S(2)}, u32[]{:S(2)}) %collective-permute-start.6) | collective-permute-done | bytes 262176 | tf_op jit(solution)/shard_map/ppermute | solution.py:19
  35.1 0.5 %collective-permute-start.18 = (bf16[128,8,128]{2,1,0:T(8,128)(2,1)S(1)}, bf16[128,8,128]{2,1,0:T(8,128)(2,1)S(1)}, u32[]{:S(2)}, u32[]{:S(2)}) collective-permute-start(bf16[128,8,128]{2,1,0:T(8,128)(2,1)S(1)} %collective-permute-done.16.refs_13_), channel_id=1, source_target_pairs={{0,1},{1,0},{2,3},{3,2},{4,5},{5,4},{6,7},{7,6},{8,9},{9,8},{10,11... | collective-permute-start | bytes 786440 | tf_op jit(solution)/shard_map/ppermute | solution.py:19
  35.7 1.0 %collective-permute-done.8.refs_7_ = bf16[128,8,128]{2,1,0:T(8,128)(2,1)S(1)} collective-permute-done((bf16[128,8,128]{2,1,0:T(8,128)(2,1)S(1)}, bf16[128,8,128]{2,1,0:T(8,128)(2,1)S(1)}, u32[]{:S(2)}, u32[]{:S(2)}) %collective-permute-start.8) | collective-permute-done | bytes 262176 | tf_op jit(solution)/shard_map/ppermute | solution.py:19
  36.6 0.4 collective-permute-done.18.refs_15_
  37.0 9.9 %aperture_sums.1 = f32[32,1024]{1,0:T(8,128)} custom-call(s32[1,2048]{1,0:T(1,128)S(1)} %fusion.2.places, s32[32,32]{1,0:T(8,128)S(1)} %bitcast.4, f32[16]{0:T(128)S(1)} %copy-done.1, bf16[128,8,128]{2,1,0:T(8,128)(2,1)S(1)} %constant_dynamic-update-slice_fusion.refs_0_, bf16[128,8,128]{2,1,0:T(8,128)(2,1)S(1)} %collective-permute-done.1.refs_1_, ...), custom_call_target="tpu_custom_call" | custom-call | tf_op jit(solution)/shard_map/aperture_sums/pallas_call | solution.py:152
  (33 shorter events, 0.2 us)
Async XLA Ops:
  0.0 8.2 %copy-start.4 = (s32[1,1024]{1,0:T(1,128)S(1)}, s32[1,1024]{1,0:T(1,128)}, u32[]{:S(2)}) copy-start(s32[1,1024]{1,0:T(1,128)} %param.7) | copy-start | bytes 12292
  0.0 8.3 %copy-start.2 = (s32[1,32,32]{2,1,0:T(8,128)S(1)}, s32[1,32,32]{2,1,0:T(8,128)}, u32[]{:S(2)}) copy-start(s32[1,32,32]{2,1,0:T(8,128)} %param.8) | copy-start | bytes 12292
  0.0 8.4 %copy-start.3 = (s32[1,32,32]{2,1,0:T(8,128)S(1)}, s32[1,32,32]{2,1,0:T(8,128)}, u32[]{:S(2)}) copy-start(s32[1,32,32]{2,1,0:T(8,128)} %param.9) | copy-start | bytes 12292
  1.0 12.4 %collective-permute-start.9 = (bf16[64,8,128]{2,1,0:T(8,128)(2,1)S(1)}, bf16[64,8,128]{2,1,0:T(8,128)(2,1)S(1)}, u32[]{:S(2)}, u32[]{:S(2)}) collective-permute-start(bf16[64,8,128]{2,1,0:T(8,128)(2,1)S(1)} %bitcast.5), channel_id=1, source_target_pairs={{0,16},{1,17},{2,18},{3,19},{4,20},{5,21},{6,22},{7,23},{8,24},{9,... | collective-permute-start | bytes 393224 | tf_op jit(solution)/shard_map/ppermute | solution.py:19
  5.1 10.2 %collective-permute-start.4 = (bf16[64,8,128]{2,1,0:T(8,128)(2,1)S(1)}, bf16[64,8,128]{2,1,0:T(8,128)(2,1)S(1)}, u32[]{:S(2)}, u32[]{:S(2)}) collective-permute-start(bf16[64,8,128]{2,1,0:T(8,128)(2,1)S(1)} %bitcast.6), channel_id=1, source_target_pairs={{0,8},{1,9},{2,10},{3,11},{4,12},{5,13},{6,14},{7,15},{8,0},{9,1},... | collective-permute-start | bytes 393224 | tf_op jit(solution)/shard_map/ppermute | solution.py:19
  6.7 5.0 %collective-permute-start = (bf16[64,8,128]{2,1,0:T(8,128)(2,1)S(1)}, bf16[64,8,128]{2,1,0:T(8,128)(2,1)S(1)}, u32[]{:S(2)}, u32[]{:S(2)}) collective-permute-start(bf16[64,8,128]{2,1,0:T(8,128)(2,1)S(1)} %bitcast.7), channel_id=1, source_target_pairs={{0,2},{1,5},{2,0},{3,7},{4,6},{5,1},{6,4},{7,3},{8,10},{9,13},{10,... | collective-permute-start | bytes 393224 | tf_op jit(solution)/shard_map/ppermute | solution.py:19
  11.7 13.2 %collective-permute-start.2 = (bf16[128,8,128]{2,1,0:T(8,128)(2,1)S(1)}, bf16[128,8,128]{2,1,0:T(8,128)(2,1)S(1)}, u32[]{:S(2)}, u32[]{:S(2)}) collective-permute-start(bf16[128,8,128]{2,1,0:T(8,128)(2,1)S(1)} %constant_dynamic-update-slice_fusion.refs_0_), channel_id=1, source_target_pairs={{0,1},{1,0},{2,3},{3,2},{4,5},{5,4},{6,7},{7,6},{8,9},{9,8},{10,11... | collective-permute-start | bytes 786440 | tf_op jit(solution)/shard_map/ppermute | solution.py:19
  11.8 14.9 %collective-permute-start.1 = (bf16[128,8,128]{2,1,0:T(8,128)(2,1)S(1)}, bf16[128,8,128]{2,1,0:T(8,128)(2,1)S(1)}, u32[]{:S(2)}, u32[]{:S(2)}) collective-permute-start(bf16[128,8,128]{2,1,0:T(8,128)(2,1)S(1)} %constant_dynamic-update-slice_fusion.refs_0_), channel_id=1, source_target_pairs={{0,4},{1,3},{2,6},{3,1},{4,0},{5,7},{6,2},{7,5},{8,12},{9,11},{10,... | collective-permute-start | bytes 786440 | tf_op jit(solution)/shard_map/ppermute | solution.py:19
  13.3 5.9 %collective-permute-start.14 = (bf16[64,8,128]{2,1,0:T(8,128)(2,1)S(1)}, bf16[64,8,128]{2,1,0:T(8,128)(2,1)S(1)}, u32[]{:S(2)}, u32[]{:S(2)}) collective-permute-start(bf16[64,8,128]{2,1,0:T(8,128)(2,1)S(1)} %collective-permute-done.9), channel_id=1, source_target_pairs={{0,8},{1,9},{2,10},{3,11},{4,12},{5,13},{6,14},{7,15},{8,0},{9,1},... | collective-permute-start | bytes 393224 | tf_op jit(solution)/shard_map/ppermute | solution.py:19
  13.8 5.3 %collective-permute-start.10 = (bf16[64,8,128]{2,1,0:T(8,128)(2,1)S(1)}, bf16[64,8,128]{2,1,0:T(8,128)(2,1)S(1)}, u32[]{:S(2)}, u32[]{:S(2)}) collective-permute-start(bf16[64,8,128]{2,1,0:T(8,128)(2,1)S(1)} %collective-permute-done.9), channel_id=1, source_target_pairs={{0,2},{1,5},{2,0},{3,7},{4,6},{5,1},{6,4},{7,3},{8,10},{9,13},{10,... | collective-permute-start | bytes 393224 | tf_op jit(solution)/shard_map/ppermute | solution.py:19
  15.3 5.5 %collective-permute-start.5 = (bf16[64,8,128]{2,1,0:T(8,128)(2,1)S(1)}, bf16[64,8,128]{2,1,0:T(8,128)(2,1)S(1)}, u32[]{:S(2)}, u32[]{:S(2)}) collective-permute-start(bf16[64,8,128]{2,1,0:T(8,128)(2,1)S(1)} %collective-permute-done.4), channel_id=1, source_target_pairs={{0,2},{1,5},{2,0},{3,7},{4,6},{5,1},{6,4},{7,3},{8,10},{9,13},{10,... | collective-permute-start | bytes 393224 | tf_op jit(solution)/shard_map/ppermute | solution.py:19
  19.1 10.7 %collective-permute-start.12 = (bf16[128,8,128]{2,1,0:T(8,128)(2,1)S(1)}, bf16[128,8,128]{2,1,0:T(8,128)(2,1)S(1)}, u32[]{:S(2)}, u32[]{:S(2)}) collective-permute-start(bf16[128,8,128]{2,1,0:T(8,128)(2,1)S(1)} %constant_dynamic-update-slice_fusion.4.refs_8_), channel_id=1, source_target_pairs={{0,1},{1,0},{2,3},{3,2},{4,5},{5,4},{6,7},{7,6},{8,9},{9,8},{10,11... | collective-permute-start | bytes 786440 | tf_op jit(solution)/shard_map/ppermute | solution.py:19
  19.2 5.6 %collective-permute-start.15 = (bf16[64,8,128]{2,1,0:T(8,128)(2,1)S(1)}, bf16[64,8,128]{2,1,0:T(8,128)(2,1)S(1)}, u32[]{:S(2)}, u32[]{:S(2)}) collective-permute-start(bf16[64,8,128]{2,1,0:T(8,128)(2,1)S(1)} %collective-permute-done.14), channel_id=1, source_target_pairs={{0,2},{1,5},{2,0},{3,7},{4,6},{5,1},{6,4},{7,3},{8,10},{9,13},{10,... | collective-permute-start | bytes 393224 | tf_op jit(solution)/shard_map/ppermute | solution.py:19
  20.7 9.1 %collective-permute-start.11 = (bf16[128,8,128]{2,1,0:T(8,128)(2,1)S(1)}, bf16[128,8,128]{2,1,0:T(8,128)(2,1)S(1)}, u32[]{:S(2)}, u32[]{:S(2)}) collective-permute-start(bf16[128,8,128]{2,1,0:T(8,128)(2,1)S(1)} %constant_dynamic-update-slice_fusion.4.refs_8_), channel_id=1, source_target_pairs={{0,4},{1,3},{2,6},{3,1},{4,0},{5,7},{6,2},{7,5},{8,12},{9,11},{10,... | collective-permute-start | bytes 786440 | tf_op jit(solution)/shard_map/ppermute | solution.py:19
  24.8 5.4 %collective-permute-start.7 = (bf16[128,8,128]{2,1,0:T(8,128)(2,1)S(1)}, bf16[128,8,128]{2,1,0:T(8,128)(2,1)S(1)}, u32[]{:S(2)}, u32[]{:S(2)}) collective-permute-start(bf16[128,8,128]{2,1,0:T(8,128)(2,1)S(1)} %constant_dynamic-update-slice_fusion.2.refs_4_), channel_id=1, source_target_pairs={{0,1},{1,0},{2,3},{3,2},{4,5},{5,4},{6,7},{7,6},{8,9},{9,8},{10,11... | collective-permute-start | bytes 786440 | tf_op jit(solution)/shard_map/ppermute | solution.py:19
  24.9 10.2 %collective-permute-start.16 = (bf16[128,8,128]{2,1,0:T(8,128)(2,1)S(1)}, bf16[128,8,128]{2,1,0:T(8,128)(2,1)S(1)}, u32[]{:S(2)}, u32[]{:S(2)}) collective-permute-start(bf16[128,8,128]{2,1,0:T(8,128)(2,1)S(1)} %constant_dynamic-update-slice_fusion.6.refs_12_), channel_id=1, source_target_pairs={{0,4},{1,3},{2,6},{3,1},{4,0},{5,7},{6,2},{7,5},{8,12},{9,11},{10,... | collective-permute-start | bytes 786440 | tf_op jit(solution)/shard_map/ppermute | solution.py:19
  26.6 8.5 %collective-permute-start.6 = (bf16[128,8,128]{2,1,0:T(8,128)(2,1)S(1)}, bf16[128,8,128]{2,1,0:T(8,128)(2,1)S(1)}, u32[]{:S(2)}, u32[]{:S(2)}) collective-permute-start(bf16[128,8,128]{2,1,0:T(8,128)(2,1)S(1)} %collective-permute-done.1.refs_1_), channel_id=1, source_target_pairs={{0,8},{1,9},{2,10},{3,11},{4,12},{5,13},{6,14},{7,15},{8,0},{9,1},... | collective-permute-start | bytes 786440 | tf_op jit(solution)/shard_map/ppermute | solution.py:19
  28.2 8.8 %copy-start = (s32[1,32,32]{2,1,0:T(8,128)S(1)}, s32[1,32,32]{2,1,0:T(8,128)}, u32[]{:S(2)}) copy-start(s32[1,32,32]{2,1,0:T(8,128)} %param.10) | copy-start | bytes 12292
  28.2 8.8 %copy-start.1 = (f32[16]{0:T(128)S(1)}, f32[16]{0:T(128)}, u32[]{:S(2)}) copy-start(f32[16]{0:T(128)} %table.1) | copy-start | bytes 196
  29.7 5.9 %collective-permute-start.17 = (bf16[128,8,128]{2,1,0:T(8,128)(2,1)S(1)}, bf16[128,8,128]{2,1,0:T(8,128)(2,1)S(1)}, u32[]{:S(2)}, u32[]{:S(2)}) collective-permute-start(bf16[128,8,128]{2,1,0:T(8,128)(2,1)S(1)} %constant_dynamic-update-slice_fusion.6.refs_12_), channel_id=1, source_target_pairs={{0,1},{1,0},{2,3},{3,2},{4,5},{5,4},{6,7},{7,6},{8,9},{9,8},{10,11... | collective-permute-start | bytes 786440 | tf_op jit(solution)/shard_map/ppermute | solution.py:19
  29.9 5.8 %collective-permute-start.3 = (bf16[128,8,128]{2,1,0:T(8,128)(2,1)S(1)}, bf16[128,8,128]{2,1,0:T(8,128)(2,1)S(1)}, u32[]{:S(2)}, u32[]{:S(2)}) collective-permute-start(bf16[128,8,128]{2,1,0:T(8,128)(2,1)S(1)} %collective-permute-done.1.refs_1_), channel_id=1, source_target_pairs={{0,1},{1,0},{2,3},{3,2},{4,5},{5,4},{6,7},{7,6},{8,9},{9,8},{10,11... | collective-permute-start | bytes 786440 | tf_op jit(solution)/shard_map/ppermute | solution.py:19
  30.2 5.4 %collective-permute-start.13 = (bf16[128,8,128]{2,1,0:T(8,128)(2,1)S(1)}, bf16[128,8,128]{2,1,0:T(8,128)(2,1)S(1)}, u32[]{:S(2)}, u32[]{:S(2)}) collective-permute-start(bf16[128,8,128]{2,1,0:T(8,128)(2,1)S(1)} %collective-permute-done.11.refs_9_), channel_id=1, source_target_pairs={{0,1},{1,0},{2,3},{3,2},{4,5},{5,4},{6,7},{7,6},{8,9},{9,8},{10,11... | collective-permute-start | bytes 786440 | tf_op jit(solution)/shard_map/ppermute | solution.py:19
  35.1 1.5 %collective-permute-start.8 = (bf16[128,8,128]{2,1,0:T(8,128)(2,1)S(1)}, bf16[128,8,128]{2,1,0:T(8,128)(2,1)S(1)}, u32[]{:S(2)}, u32[]{:S(2)}) collective-permute-start(bf16[128,8,128]{2,1,0:T(8,128)(2,1)S(1)} %collective-permute-done.6.refs_5_), channel_id=1, source_target_pairs={{0,1},{1,0},{2,3},{3,2},{4,5},{5,4},{6,7},{7,6},{8,9},{9,8},{10,11... | collective-permute-start | bytes 786440 | tf_op jit(solution)/shard_map/ppermute | solution.py:19
  35.1 1.9 %collective-permute-start.18 = (bf16[128,8,128]{2,1,0:T(8,128)(2,1)S(1)}, bf16[128,8,128]{2,1,0:T(8,128)(2,1)S(1)}, u32[]{:S(2)}, u32[]{:S(2)}) collective-permute-start(bf16[128,8,128]{2,1,0:T(8,128)(2,1)S(1)} %collective-permute-done.16.refs_13_), channel_id=1, source_target_pairs={{0,1},{1,0},{2,3},{3,2},{4,5},{5,4},{6,7},{7,6},{8,9},{9,8},{10,11... | collective-permute-start | bytes 786440 | tf_op jit(solution)/shard_map/ppermute | solution.py:19
where the time goes:
time: 47 us; the launch traced here: 46.9 us
  starting transfers between devices  19.1 us (41%)
  waiting for transfers between devices  15 us (32%)
  Pallas kernels  9.89 us (21%)
  matrix products  1.52 us (3%)
  local copies, waits for them, and re-layouts  1.24 us (3%)
    ppermute x19, starting transfers between devices, exchange(): lax.ppermute(value, 'dev', [(i, i ^ (odd if i & 1 else even)) for i in ra...  19.1 us
    ppermute x19, waiting for transfers between devices, exchange(): lax.ppermute(value, 'dev', [(i, i ^ (odd if i & 1 else even)) for i in ra...  15 us
    pallas_call x1, Pallas kernels, aperture_sums(): pl.pallas_call(functools.partial(aperture_kernel, [slot * rows_each for _...  9.89 us
    dot_general x1, matrix products, shards(): jnp.dot(digits, (listed == wanted).astype(jnp.bfloat16), preferred_elemen...  1.52 us
    unnamed x15, local copies, waits for them, and re-layouts  1.01 us
  transfers between devices with their start and end apart: 19, of which 6 were waited for; matrix products, arithmetic and copies ran while one was open for 4% of the time, Pallas kernels for 0%

commit v1 on v0

--- a/solution.py
+++ b/solution.py
@@ -19,15 +19,25 @@
     return lax.ppermute(value, "dev", [(i, i ^ (odd if i & 1 else even)) for i in range(count)])
 
 
-def gather_blocks(own, count):
-    levels = {0: own}
+def tiles_of(rows):
+    return rows.reshape(rows.shape[0], rows.shape[1] // LANES, LANES)
+
+
+def gather_blocks(traces, count):
+    rows = {0: traces}
+    levels = {}
     fars = []
     pieces = []
 
+    def rows_of(level):
+        if level not in rows:
+            low = level & -level
+            rows[level] = exchange(rows_of(level ^ low), count, 8 * low)
+        return rows[level]
+
     def level_of(level):
         if level not in levels:
-            low = level & -level
-            levels[level] = exchange(level_of(level ^ low), count, 8 * low)
+            levels[level] = exchange(level_of(0), count, 8) if level == 1 else tiles_of(rows_of(level))
         return levels[level]
 
     for level in range(count // 8):
@@ -178,7 +188,7 @@
     rows_each, samples = traces.shape
     count = lax.axis_size("dev")
     _, aperture = pair_left.shape[1:]
-    pieces = gather_blocks(traces.reshape(rows_each, samples // LANES, LANES), count)
+    pieces = gather_blocks(traces, count)
 
     slot, row = slots_of(fetch_rows, rows_each, count)
     digits = jnp.concatenate([slot, row], axis=0).astype(jnp.bfloat16)

time: 47 us -> 47.8 us (1.017)
  waiting for transfers between devices: 15 us -> 20.3 us
  starting transfers between devices: 19.1 us -> 14.3 us
    ppermute x19, waiting for transfers between devices: 15 us -> 20.3 us  [exchange(): lax.ppermute(value, 'dev', [(i, i ^ (odd if i & 1 else even)) for i in ra...]
    ppermute x19, starting transfers between devices: 19.1 us -> 14.3 us  [exchange(): lax.ppermute(value, 'dev', [(i, i ^ (odd if i & 1 else even)) for i in ra...]
    unnamed x15 -> x19, local copies, waits for them, and re-layouts: 1.01 us -> 1.09 us
  transfers between devices with their start and end apart: 19 -> 19, of which waited for: 6 -> 7; matrix products, arithmetic and copies ran while one was open for 4% -> 4% of each run, Pallas kernels for 0% -> 0%
where the time goes in v1:
time: 47.8 us; the launch traced here: 47.6 us
  waiting for transfers between devices  20.3 us (42%)
  starting transfers between devices  14.3 us (30%)
  Pallas kernels  9.88 us (21%)
  matrix products  1.52 us (3%)
  local copies, waits for them, and re-layouts  1.32 us (3%)
    ppermute x19, waiting for transfers between devices, exchange(): lax.ppermute(value, 'dev', [(i, i ^ (odd if i & 1 else even)) for i in ra...  20.3 us
    ppermute x19, starting transfers between devices, exchange(): lax.ppermute(value, 'dev', [(i, i ^ (odd if i & 1 else even)) for i in ra...  14.3 us
    pallas_call x1, Pallas kernels, aperture_sums(): pl.pallas_call(functools.partial(aperture_kernel, [slot * rows_each for _...  9.88 us
    dot_general x1, matrix products, shards(): jnp.dot(digits, (listed == wanted).astype(jnp.bfloat16), preferred_elemen...  1.52 us
    unnamed x19, local copies, waits for them, and re-layouts  1.09 us
  transfers between devices with their start and end apart: 19, of which 7 were waited for; matrix products, arithmetic and copies ran while one was open for 4% of the time, Pallas kernels for 0%

profile of v1, /device:TPU:0, one launch (start us, length us, event | category | flops | bytes accessed | tf_op | source)
XLA Modules:
  0.0 47.6 jit_solution(10434582918297608089)
XLA Ops:
  0.0 1.0 %copy.7 = bf16[8,8,8,128]{3,2,1,0:T(8,128)(2,1)S(1)} copy(bf16[8,8,8,128]{3,1,2,0:T(8,128)(2,1)} %bitcast.16) | data formatting | bytes 262144
  1.0 3.1 %collective-permute-start.4 = (bf16[64,8,128]{2,1,0:T(8,128)(2,1)S(1)}, bf16[64,8,128]{2,1,0:T(8,128)(2,1)S(1)}, u32[]{:S(2)}, u32[]{:S(2)}) collective-permute-start(bf16[64,8,128]{2,1,0:T(8,128)(2,1)S(1)} %bitcast.9), channel_id=1, source_target_pairs={{0,8},{1,9},{2,10},{3,11},{4,12},{5,13},{6,14},{7,15},{8,0},{9,1},... | collective-permute-start | bytes 393224 | tf_op jit(solution)/shard_map/ppermute | solution.py:19
  4.1 1.5 %collective-permute-start = (bf16[64,8,128]{2,1,0:T(8,128)(2,1)S(1)}, bf16[64,8,128]{2,1,0:T(8,128)(2,1)S(1)}, u32[]{:S(2)}, u32[]{:S(2)}) collective-permute-start(bf16[64,8,128]{2,1,0:T(8,128)(2,1)S(1)} %bitcast.10), channel_id=1, source_target_pairs={{0,2},{1,5},{2,0},{3,7},{4,6},{5,1},{6,4},{7,3},{8,10},{9,13},{10,... | collective-permute-start | bytes 393224 | tf_op jit(solution)/shard_map/ppermute | solution.py:19
  5.6 2.6 %collective-permute-start.9 = (bf16[64,1024]{1,0:T(8,128)(2,1)S(1)}, bf16[64,1024]{1,0:T(8,128)(2,1)S(1)}, u32[]{:S(2)}, u32[]{:S(2)}) collective-permute-start(bf16[64,1024]{1,0:T(8,128)(2,1)S(1)} %copy-done.2), channel_id=1, source_target_pairs={{0,16},{1,17},{2,18},{3,19},{4,20},{5,21},{6,22},{7,23},{8,24},{9,... | collective-permute-start | bytes 393224 | tf_op jit(solution)/shard_map/ppermute | solution.py:19
  8.2 0.1 add_convert_fusion
  8.3 0.1 reshape.15
  8.4 0.1 reshape.16
  8.5 5.6 %collective-permute-done.9 = bf16[64,1024]{1,0:T(8,128)(2,1)S(1)} collective-permute-done((bf16[64,1024]{1,0:T(8,128)(2,1)S(1)}, bf16[64,1024]{1,0:T(8,128)(2,1)S(1)}, u32[]{:S(2)}, u32[]{:S(2)}) %collective-permute-start.9) | collective-permute-done | bytes 131104 | tf_op jit(solution)/shard_map/ppermute | solution.py:19
  14.1 1.6 %collective-permute-start.10 = (bf16[64,8,128]{2,1,0:T(8,128)(2,1)S(1)}, bf16[64,8,128]{2,1,0:T(8,128)(2,1)S(1)}, u32[]{:S(2)}, u32[]{:S(2)}) collective-permute-start(bf16[64,8,128]{2,1,0:T(8,128)(2,1)S(1)} %bitcast.12), channel_id=1, source_target_pairs={{0,2},{1,5},{2,0},{3,7},{4,6},{5,1},{6,4},{7,3},{8,10},{9,13},{10,... | collective-permute-start | bytes 393224 | tf_op jit(solution)/shard_map/ppermute | solution.py:19
  15.6 0.1 collective-permute-start.14
  15.7 0.1 collective-permute-start.2
  15.8 0.8 %collective-permute-start.1 = (bf16[128,8,128]{2,1,0:T(8,128)(2,1)S(1)}, bf16[128,8,128]{2,1,0:T(8,128)(2,1)S(1)}, u32[]{:S(2)}, u32[]{:S(2)}) collective-permute-start(bf16[128,8,128]{2,1,0:T(8,128)(2,1)S(1)} %constant_dynamic-update-slice_fusion.refs_0_), channel_id=1, source_target_pairs={{0,4},{1,3},{2,6},{3,1},{4,0},{5,7},{6,2},{7,5},{8,12},{9,11},{10,... | collective-permute-start | bytes 786440 | tf_op jit(solution)/shard_map/ppermute | solution.py:19
  16.6 0.9 %collective-permute-start.5 = (bf16[64,8,128]{2,1,0:T(8,128)(2,1)S(1)}, bf16[64,8,128]{2,1,0:T(8,128)(2,1)S(1)}, u32[]{:S(2)}, u32[]{:S(2)}) collective-permute-start(bf16[64,8,128]{2,1,0:T(8,128)(2,1)S(1)} %collective-permute-done.4), channel_id=1, source_target_pairs={{0,2},{1,5},{2,0},{3,7},{4,6},{5,1},{6,4},{7,3},{8,10},{9,13},{10,... | collective-permute-start | bytes 393224 | tf_op jit(solution)/shard_map/ppermute | solution.py:19
  17.5 3.1 %collective-permute-done.14 = bf16[64,1024]{1,0:T(8,128)(2,1)S(1)} collective-permute-done((bf16[64,1024]{1,0:T(8,128)(2,1)S(1)}, bf16[64,1024]{1,0:T(8,128)(2,1)S(1)}, u32[]{:S(2)}, u32[]{:S(2)}) %collective-permute-start.14) | collective-permute-done | bytes 131104 | tf_op jit(solution)/shard_map/ppermute | solution.py:19
  20.7 0.6 %collective-permute-start.15 = (bf16[64,8,128]{2,1,0:T(8,128)(2,1)S(1)}, bf16[64,8,128]{2,1,0:T(8,128)(2,1)S(1)}, u32[]{:S(2)}, u32[]{:S(2)}) collective-permute-start(bf16[64,8,128]{2,1,0:T(8,128)(2,1)S(1)} %bitcast.14), channel_id=1, source_target_pairs={{0,2},{1,5},{2,0},{3,7},{4,6},{5,1},{6,4},{7,3},{8,10},{9,13},{10,... | collective-permute-start | bytes 393224 | tf_op jit(solution)/shard_map/ppermute | solution.py:19
  21.3 0.1 collective-permute-start.12
  21.4 1.6 %collective-permute-done.5 = bf16[64,8,128]{2,1,0:T(8,128)(2,1)S(1)} collective-permute-done((bf16[64,8,128]{2,1,0:T(8,128)(2,1)S(1)}, bf16[64,8,128]{2,1,0:T(8,128)(2,1)S(1)}, u32[]{:S(2)}, u32[]{:S(2)}) %collective-permute-start.5) | collective-permute-done | bytes 131104 | tf_op jit(solution)/shard_map/ppermute | solution.py:19
  23.0 1.3 %collective-permute-start.11 = (bf16[128,8,128]{2,1,0:T(8,128)(2,1)S(1)}, bf16[128,8,128]{2,1,0:T(8,128)(2,1)S(1)}, u32[]{:S(2)}, u32[]{:S(2)}) collective-permute-start(bf16[128,8,128]{2,1,0:T(8,128)(2,1)S(1)} %constant_dynamic-update-slice_fusion.4.refs_8_), channel_id=1, source_target_pairs={{0,4},{1,3},{2,6},{3,1},{4,0},{5,7},{6,2},{7,5},{8,12},{9,11},{10,... | collective-permute-start | bytes 786440 | tf_op jit(solution)/shard_map/ppermute | solution.py:19
  24.3 2.6 %collective-permute-done.15 = bf16[64,8,128]{2,1,0:T(8,128)(2,1)S(1)} collective-permute-done((bf16[64,8,128]{2,1,0:T(8,128)(2,1)S(1)}, bf16[64,8,128]{2,1,0:T(8,128)(2,1)S(1)}, u32[]{:S(2)}, u32[]{:S(2)}) %collective-permute-start.15) | collective-permute-done | bytes 131104 | tf_op jit(solution)/shard_map/ppermute | solution.py:19
  26.9 0.0 collective-permute-start.7
  26.9 0.0 collective-permute-done.2.refs_2_
  27.0 0.1 collective-permute-start.16
  27.0 0.0 collective-permute-done.1.refs_1_
  27.0 0.6 %collective-permute-start.6 = (bf16[128,8,128]{2,1,0:T(8,128)(2,1)S(1)}, bf16[128,8,128]{2,1,0:T(8,128)(2,1)S(1)}, u32[]{:S(2)}, u32[]{:S(2)}) collective-permute-start(bf16[128,8,128]{2,1,0:T(8,128)(2,1)S(1)} %collective-permute-done.1.refs_1_), channel_id=1, source_target_pairs={{0,8},{1,9},{2,10},{3,11},{4,12},{5,13},{6,14},{7,15},{8,0},{9,1},... | collective-permute-start | bytes 786440 | tf_op jit(solution)/shard_map/ppermute | solution.py:19
  27.7 1.5 %fusion = f32[2,2048]{1,0:T(2,128)S(1)} fusion(s32[2048]{0:T(1024)S(1)} %bitcast.19, bf16[1,1024]{1,0:T(2,128)(2,1)S(1)} %fusion.3, bf16[1,1024]{1,0:T(2,128)(2,1)S(1)} %get-tuple-element.5), kind=kOutput, calls=%fused_computation.1 | convolution fusion | flops 10493952 | bytes 28672 | tf_op jit(solution)/shard_map/dot_general | solution.py:197
  29.2 0.5 %collective-permute-start.3 = (bf16[128,8,128]{2,1,0:T(8,128)(2,1)S(1)}, bf16[128,8,128]{2,1,0:T(8,128)(2,1)S(1)}, u32[]{:S(2)}, u32[]{:S(2)}) collective-permute-start(bf16[128,8,128]{2,1,0:T(8,128)(2,1)S(1)} %collective-permute-done.1.refs_1_), channel_id=1, source_target_pairs={{0,1},{1,0},{2,3},{3,2},{4,5},{5,4},{6,7},{7,6},{8,9},{9,8},{10,11... | collective-permute-start | bytes 786440 | tf_op jit(solution)/shard_map/ppermute | solution.py:19
  29.7 0.1 collective-permute-start.13
  29.8 6.0 %collective-permute-done.6.refs_5_ = bf16[128,8,128]{2,1,0:T(8,128)(2,1)S(1)} collective-permute-done((bf16[128,8,128]{2,1,0:T(8,128)(2,1)S(1)}, bf16[128,8,128]{2,1,0:T(8,128)(2,1)S(1)}, u32[]{:S(2)}, u32[]{:S(2)}) %collective-permute-start.6) | collective-permute-done | bytes 262176 | tf_op jit(solution)/shard_map/ppermute | solution.py:19
  35.8 0.5 %collective-permute-start.18 = (bf16[128,8,128]{2,1,0:T(8,128)(2,1)S(1)}, bf16[128,8,128]{2,1,0:T(8,128)(2,1)S(1)}, u32[]{:S(2)}, u32[]{:S(2)}) collective-permute-start(bf16[128,8,128]{2,1,0:T(8,128)(2,1)S(1)} %collective-permute-done.16.refs_13_), channel_id=1, source_target_pairs={{0,1},{1,0},{2,3},{3,2},{4,5},{5,4},{6,7},{7,6},{8,9},{9,8},{10,11... | collective-permute-start | bytes 786440 | tf_op jit(solution)/shard_map/ppermute | solution.py:19
  36.4 1.0 %collective-permute-done.8.refs_7_ = bf16[128,8,128]{2,1,0:T(8,128)(2,1)S(1)} collective-permute-done((bf16[128,8,128]{2,1,0:T(8,128)(2,1)S(1)}, bf16[128,8,128]{2,1,0:T(8,128)(2,1)S(1)}, u32[]{:S(2)}, u32[]{:S(2)}) %collective-permute-start.8) | collective-permute-done | bytes 262176 | tf_op jit(solution)/shard_map/ppermute | solution.py:19
  37.4 0.4 collective-permute-done.18.refs_15_
  37.7 9.9 %aperture_sums.1 = f32[32,1024]{1,0:T(8,128)} custom-call(s32[1,2048]{1,0:T(1,128)S(1)} %fusion.2.places, s32[32,32]{1,0:T(8,128)S(1)} %bitcast.8, f32[16]{0:T(128)S(1)} %copy-done.1, bf16[128,8,128]{2,1,0:T(8,128)(2,1)S(1)} %constant_dynamic-update-slice_fusion.refs_0_, bf16[128,8,128]{2,1,0:T(8,128)(2,1)S(1)} %collective-permute-done.1.refs_1_, ...), custom_call_target="tpu_custom_call" | custom-call | tf_op jit(solution)/shard_map/aperture_sums/pallas_call | solution.py:162
  (37 shorter events, 0.2 us)
Async XLA Ops:
  0.0 5.6 %copy-start.2 = (bf16[64,1024]{1,0:T(8,128)(2,1)S(1)}, bf16[64,1024]{1,0:T(8,128)(2,1)}, u32[]{:S(2)}) copy-start(bf16[64,1024]{1,0:T(8,128)(2,1)} %param.6) | copy-start | bytes 393220
  0.0 8.2 %copy-start.5 = (s32[1,1024]{1,0:T(1,128)S(1)}, s32[1,1024]{1,0:T(1,128)}, u32[]{:S(2)}) copy-start(s32[1,1024]{1,0:T(1,128)} %param.7) | copy-start | bytes 12292
  0.0 8.3 %copy-start.3 = (s32[1,32,32]{2,1,0:T(8,128)S(1)}, s32[1,32,32]{2,1,0:T(8,128)}, u32[]{:S(2)}) copy-start(s32[1,32,32]{2,1,0:T(8,128)} %param.8) | copy-start | bytes 12292
  0.0 8.4 %copy-start.4 = (s32[1,32,32]{2,1,0:T(8,128)S(1)}, s32[1,32,32]{2,1,0:T(8,128)}, u32[]{:S(2)}) copy-start(s32[1,32,32]{2,1,0:T(8,128)} %param.9) | copy-start | bytes 12292
  1.0 15.6 %collective-permute-start.4 = (bf16[64,8,128]{2,1,0:T(8,128)(2,1)S(1)}, bf16[64,8,128]{2,1,0:T(8,128)(2,1)S(1)}, u32[]{:S(2)}, u32[]{:S(2)}) collective-permute-start(bf16[64,8,128]{2,1,0:T(8,128)(2,1)S(1)} %bitcast.9), channel_id=1, source_target_pairs={{0,8},{1,9},{2,10},{3,11},{4,12},{5,13},{6,14},{7,15},{8,0},{9,1},... | collective-permute-start | bytes 393224 | tf_op jit(solution)/shard_map/ppermute | solution.py:19
  4.1 11.6 %collective-permute-start = (bf16[64,8,128]{2,1,0:T(8,128)(2,1)S(1)}, bf16[64,8,128]{2,1,0:T(8,128)(2,1)S(1)}, u32[]{:S(2)}, u32[]{:S(2)}) collective-permute-start(bf16[64,8,128]{2,1,0:T(8,128)(2,1)S(1)} %bitcast.10), channel_id=1, source_target_pairs={{0,2},{1,5},{2,0},{3,7},{4,6},{5,1},{6,4},{7,3},{8,10},{9,13},{10,... | collective-permute-start | bytes 393224 | tf_op jit(solution)/shard_map/ppermute | solution.py:19
  5.6 8.4 %collective-permute-start.9 = (bf16[64,1024]{1,0:T(8,128)(2,1)S(1)}, bf16[64,1024]{1,0:T(8,128)(2,1)S(1)}, u32[]{:S(2)}, u32[]{:S(2)}) collective-permute-start(bf16[64,1024]{1,0:T(8,128)(2,1)S(1)} %copy-done.2), channel_id=1, source_target_pairs={{0,16},{1,17},{2,18},{3,19},{4,20},{5,21},{6,22},{7,23},{8,24},{9,... | collective-permute-start | bytes 393224 | tf_op jit(solution)/shard_map/ppermute | solution.py:19
  14.1 7.2 %collective-permute-start.10 = (bf16[64,8,128]{2,1,0:T(8,128)(2,1)S(1)}, bf16[64,8,128]{2,1,0:T(8,128)(2,1)S(1)}, u32[]{:S(2)}, u32[]{:S(2)}) collective-permute-start(bf16[64,8,128]{2,1,0:T(8,128)(2,1)S(1)} %bitcast.12), channel_id=1, source_target_pairs={{0,2},{1,5},{2,0},{3,7},{4,6},{5,1},{6,4},{7,3},{8,10},{9,13},{10,... | collective-permute-start | bytes 393224 | tf_op jit(solution)/shard_map/ppermute | solution.py:19
  15.6 5.0 %collective-permute-start.14 = (bf16[64,1024]{1,0:T(8,128)(2,1)S(1)}, bf16[64,1024]{1,0:T(8,128)(2,1)S(1)}, u32[]{:S(2)}, u32[]{:S(2)}) collective-permute-start(bf16[64,1024]{1,0:T(8,128)(2,1)S(1)} %collective-permute-done.9), channel_id=1, source_target_pairs={{0,8},{1,9},{2,10},{3,11},{4,12},{5,13},{6,14},{7,15},{8,0},{9,1},... | collective-permute-start | bytes 393224 | tf_op jit(solution)/shard_map/ppermute | solution.py:19
  15.7 11.2 %collective-permute-start.2 = (bf16[128,8,128]{2,1,0:T(8,128)(2,1)S(1)}, bf16[128,8,128]{2,1,0:T(8,128)(2,1)S(1)}, u32[]{:S(2)}, u32[]{:S(2)}) collective-permute-start(bf16[128,8,128]{2,1,0:T(8,128)(2,1)S(1)} %constant_dynamic-update-slice_fusion.refs_0_), channel_id=1, source_target_pairs={{0,1},{1,0},{2,3},{3,2},{4,5},{5,4},{6,7},{7,6},{8,9},{9,8},{10,11... | collective-permute-start | bytes 786440 | tf_op jit(solution)/shard_map/ppermute | solution.py:19
  15.8 11.2 %collective-permute-start.1 = (bf16[128,8,128]{2,1,0:T(8,128)(2,1)S(1)}, bf16[128,8,128]{2,1,0:T(8,128)(2,1)S(1)}, u32[]{:S(2)}, u32[]{:S(2)}) collective-permute-start(bf16[128,8,128]{2,1,0:T(8,128)(2,1)S(1)} %constant_dynamic-update-slice_fusion.refs_0_), channel_id=1, source_target_pairs={{0,4},{1,3},{2,6},{3,1},{4,0},{5,7},{6,2},{7,5},{8,12},{9,11},{10,... | collective-permute-start | bytes 786440 | tf_op jit(solution)/shard_map/ppermute | solution.py:19
  16.6 6.4 %collective-permute-start.5 = (bf16[64,8,128]{2,1,0:T(8,128)(2,1)S(1)}, bf16[64,8,128]{2,1,0:T(8,128)(2,1)S(1)}, u32[]{:S(2)}, u32[]{:S(2)}) collective-permute-start(bf16[64,8,128]{2,1,0:T(8,128)(2,1)S(1)} %collective-permute-done.4), channel_id=1, source_target_pairs={{0,2},{1,5},{2,0},{3,7},{4,6},{5,1},{6,4},{7,3},{8,10},{9,13},{10,... | collective-permute-start | bytes 393224 | tf_op jit(solution)/shard_map/ppermute | solution.py:19
  20.7 6.2 %collective-permute-start.15 = (bf16[64,8,128]{2,1,0:T(8,128)(2,1)S(1)}, bf16[64,8,128]{2,1,0:T(8,128)(2,1)S(1)}, u32[]{:S(2)}, u32[]{:S(2)}) collective-permute-start(bf16[64,8,128]{2,1,0:T(8,128)(2,1)S(1)} %bitcast.14), channel_id=1, source_target_pairs={{0,2},{1,5},{2,0},{3,7},{4,6},{5,1},{6,4},{7,3},{8,10},{9,13},{10,... | collective-permute-start | bytes 393224 | tf_op jit(solution)/shard_map/ppermute | solution.py:19
  21.3 7.9 %collective-permute-start.12 = (bf16[128,8,128]{2,1,0:T(8,128)(2,1)S(1)}, bf16[128,8,128]{2,1,0:T(8,128)(2,1)S(1)}, u32[]{:S(2)}, u32[]{:S(2)}) collective-permute-start(bf16[128,8,128]{2,1,0:T(8,128)(2,1)S(1)} %constant_dynamic-update-slice_fusion.4.refs_8_), channel_id=1, source_target_pairs={{0,1},{1,0},{2,3},{3,2},{4,5},{5,4},{6,7},{7,6},{8,9},{9,8},{10,11... | collective-permute-start | bytes 786440 | tf_op jit(solution)/shard_map/ppermute | solution.py:19
  23.0 6.7 %collective-permute-start.11 = (bf16[128,8,128]{2,1,0:T(8,128)(2,1)S(1)}, bf16[128,8,128]{2,1,0:T(8,128)(2,1)S(1)}, u32[]{:S(2)}, u32[]{:S(2)}) collective-permute-start(bf16[128,8,128]{2,1,0:T(8,128)(2,1)S(1)} %constant_dynamic-update-slice_fusion.4.refs_8_), channel_id=1, source_target_pairs={{0,4},{1,3},{2,6},{3,1},{4,0},{5,7},{6,2},{7,5},{8,12},{9,11},{10,... | collective-permute-start | bytes 786440 | tf_op jit(solution)/shard_map/ppermute | solution.py:19
  26.9 2.3 %collective-permute-start.7 = (bf16[128,8,128]{2,1,0:T(8,128)(2,1)S(1)}, bf16[128,8,128]{2,1,0:T(8,128)(2,1)S(1)}, u32[]{:S(2)}, u32[]{:S(2)}) collective-permute-start(bf16[128,8,128]{2,1,0:T(8,128)(2,1)S(1)} %constant_dynamic-update-slice_fusion.2.refs_4_), channel_id=1, source_target_pairs={{0,1},{1,0},{2,3},{3,2},{4,5},{5,4},{6,7},{7,6},{8,9},{9,8},{10,11... | collective-permute-start | bytes 786440 | tf_op jit(solution)/shard_map/ppermute | solution.py:19
  27.0 8.9 %collective-permute-start.16 = (bf16[128,8,128]{2,1,0:T(8,128)(2,1)S(1)}, bf16[128,8,128]{2,1,0:T(8,128)(2,1)S(1)}, u32[]{:S(2)}, u32[]{:S(2)}) collective-permute-start(bf16[128,8,128]{2,1,0:T(8,128)(2,1)S(1)} %constant_dynamic-update-slice_fusion.6.refs_12_), channel_id=1, source_target_pairs={{0,4},{1,3},{2,6},{3,1},{4,0},{5,7},{6,2},{7,5},{8,12},{9,11},{10,... | collective-permute-start | bytes 786440 | tf_op jit(solution)/shard_map/ppermute | solution.py:19
  27.0 8.8 %collective-permute-start.6 = (bf16[128,8,128]{2,1,0:T(8,128)(2,1)S(1)}, bf16[128,8,128]{2,1,0:T(8,128)(2,1)S(1)}, u32[]{:S(2)}, u32[]{:S(2)}) collective-permute-start(bf16[128,8,128]{2,1,0:T(8,128)(2,1)S(1)} %collective-permute-done.1.refs_1_), channel_id=1, source_target_pairs={{0,8},{1,9},{2,10},{3,11},{4,12},{5,13},{6,14},{7,15},{8,0},{9,1},... | collective-permute-start | bytes 786440 | tf_op jit(solution)/shard_map/ppermute | solution.py:19
  27.7 10.1 %copy-start = (s32[1,32,32]{2,1,0:T(8,128)S(1)}, s32[1,32,32]{2,1,0:T(8,128)}, u32[]{:S(2)}) copy-start(s32[1,32,32]{2,1,0:T(8,128)} %param.10) | copy-start | bytes 12292
  27.7 10.1 %copy-start.1 = (f32[16]{0:T(128)S(1)}, f32[16]{0:T(128)}, u32[]{:S(2)}) copy-start(f32[16]{0:T(128)} %table.1) | copy-start | bytes 196
  29.2 7.2 %collective-permute-start.17 = (bf16[128,8,128]{2,1,0:T(8,128)(2,1)S(1)}, bf16[128,8,128]{2,1,0:T(8,128)(2,1)S(1)}, u32[]{:S(2)}, u32[]{:S(2)}) collective-permute-start(bf16[128,8,128]{2,1,0:T(8,128)(2,1)S(1)} %constant_dynamic-update-slice_fusion.6.refs_12_), channel_id=1, source_target_pairs={{0,1},{1,0},{2,3},{3,2},{4,5},{5,4},{6,7},{7,6},{8,9},{9,8},{10,11... | collective-permute-start | bytes 786440 | tf_op jit(solution)/shard_map/ppermute | solution.py:19
  29.2 7.1 %collective-permute-start.3 = (bf16[128,8,128]{2,1,0:T(8,128)(2,1)S(1)}, bf16[128,8,128]{2,1,0:T(8,128)(2,1)S(1)}, u32[]{:S(2)}, u32[]{:S(2)}) collective-permute-start(bf16[128,8,128]{2,1,0:T(8,128)(2,1)S(1)} %collective-permute-done.1.refs_1_), channel_id=1, source_target_pairs={{0,1},{1,0},{2,3},{3,2},{4,5},{5,4},{6,7},{7,6},{8,9},{9,8},{10,11... | collective-permute-start | bytes 786440 | tf_op jit(solution)/shard_map/ppermute | solution.py:19
  29.7 6.7 %collective-permute-start.13 = (bf16[128,8,128]{2,1,0:T(8,128)(2,1)S(1)}, bf16[128,8,128]{2,1,0:T(8,128)(2,1)S(1)}, u32[]{:S(2)}, u32[]{:S(2)}) collective-permute-start(bf16[128,8,128]{2,1,0:T(8,128)(2,1)S(1)} %collective-permute-done.11.refs_9_), channel_id=1, source_target_pairs={{0,1},{1,0},{2,3},{3,2},{4,5},{5,4},{6,7},{7,6},{8,9},{9,8},{10,11... | collective-permute-start | bytes 786440 | tf_op jit(solution)/shard_map/ppermute | solution.py:19
  35.8 1.5 %collective-permute-start.8 = (bf16[128,8,128]{2,1,0:T(8,128)(2,1)S(1)}, bf16[128,8,128]{2,1,0:T(8,128)(2,1)S(1)}, u32[]{:S(2)}, u32[]{:S(2)}) collective-permute-start(bf16[128,8,128]{2,1,0:T(8,128)(2,1)S(1)} %collective-permute-done.6.refs_5_), channel_id=1, source_target_pairs={{0,1},{1,0},{2,3},{3,2},{4,5},{5,4},{6,7},{7,6},{8,9},{9,8},{10,11... | collective-permute-start | bytes 786440 | tf_op jit(solution)/shard_map/ppermute | solution.py:19
  35.8 1.9 %collective-permute-start.18 = (bf16[128,8,128]{2,1,0:T(8,128)(2,1)S(1)}, bf16[128,8,128]{2,1,0:T(8,128)(2,1)S(1)}, u32[]{:S(2)}, u32[]{:S(2)}) collective-permute-start(bf16[128,8,128]{2,1,0:T(8,128)(2,1)S(1)} %collective-permute-done.16.refs_13_), channel_id=1, source_target_pairs={{0,1},{1,0},{2,3},{3,2},{4,5},{5,4},{6,7},{7,6},{8,9},{9,8},{10,11... | collective-permute-start | bytes 786440 | tf_op jit(solution)/shard_map/ppermute | solution.py:19
